TPU v7x, 256 devices: a whole 4x4x8 slice. The times are simulated.
256 devices in a mesh: hid: 4 (over x_lo, core), tok: 64 (over x_hi, y, z).
Axes of the slice: x: 4 (x_hi: 2, x_lo: 2; x = x_hi * 2 + x_lo), y: 4, z: 8, core: 2. Of those that a mesh axis runs over, the one named last changes fastest.
Arguments:
- val_inputs: bfloat16 [256, 4096], P(None, 'tok'), may hold values from -6 to 6
- val_out_grad: bfloat16 [256, 4096], P(None, 'tok'), may hold values from -6 to 6
- w_gate: bfloat16 [4096, 14336], P('tok', 'hid'), may hold values from -0.09375 to 0.09375
- w_up: bfloat16 [4096, 14336], P('tok', 'hid'), may hold values from -0.09375 to 0.09375
- w_down: bfloat16 [14336, 4096], P('hid', 'tok'), may hold values from -0.046875 to 0.046875
- val_attn_inputs: bfloat16 [256, 4096], P('hid', 'tok'), may hold values from -6 to 6
- train_inputs: bfloat16 [163840, 4096], P(('hid', 'tok')), may hold values from -6 to 6
- train_grads: bfloat16 [163840, 4096], P(('hid', 'tok')), may hold values from -6 to 6
Outputs:
- influence: float32 [163840], P(('hid', 'tok'))
- val_grad: bfloat16 [256, 4096], P('hid', 'tok')
All inputs are finite; a program needn't handle non-finite values.
Results may differ from a plain program's by a relative error of at most 0.0036.
Values may be sent and summed in bfloat16 or wider, within the bound.
No kernel may reach another device: no remote copies, remote signals or barrier semaphores. Data moves between devices by JAX's collectives and lax.ppermute only.
A program may use at most 128 MiB of HBM per device.

v0:
```python
import math
import jax
import jax.numpy as jnp
from jax import lax
from jax.sharding import PartitionSpec as P


def dot_rows(left, right):
    return lax.dot_general(
        left, right, (((1,), (1,)), ((), ())), preferred_element_type=jnp.float32
    )


def act_grads(gate_pre, up_pre, hid_grad):
    logistic = jax.nn.sigmoid(gate_pre)
    grad_gate = (hid_grad * up_pre * logistic * (1.0 + gate_pre * (1.0 - logistic))).astype(
        jnp.bfloat16
    )
    grad_up = (hid_grad * gate_pre * logistic).astype(jnp.bfloat16)
    return (grad_gate, grad_up)


def pair_terms(train_in, train_gr, val_in, val_gr):
    in_gram = dot_rows(train_in, val_in)
    grad_gram = dot_rows(train_gr, val_gr)
    return jnp.sum(in_gram * grad_gram, axis=1)


def local(
    val_inputs, val_out_grad, w_gate, w_up, w_down, val_attn_inputs, train_inputs, train_grads
):
    hid_units = w_gate.shape[1]
    val_count = val_out_grad.shape[0]
    gate_pre = jnp.dot(val_inputs, w_gate, preferred_element_type=jnp.float32)
    up_pre = jnp.dot(val_inputs, w_up, preferred_element_type=jnp.float32)
    hid_grad = dot_rows(val_out_grad, w_down)
    sums = lax.psum_scatter(
        jnp.concatenate([gate_pre, up_pre, hid_grad], axis=1),
        "tok",
        scatter_dimension=0,
        tiled=True,
    )
    grad_gate, grad_up = act_grads(
        sums[:, :hid_units], sums[:, hid_units : 2 * hid_units], sums[:, 2 * hid_units :]
    )
    stacked = jnp.concatenate([grad_gate, grad_up], axis=1)
    piece = lax.all_gather(stacked, "tok", axis=0, tiled=True)
    dx_part = dot_rows(piece[:, :hid_units], w_gate) + dot_rows(piece[:, hid_units:], w_up)
    quarter = val_count // lax.axis_size("hid")
    first_row = lax.axis_index("hid") * quarter
    dx_rows = lax.psum_scatter(dx_part, "hid", scatter_dimension=0, tiled=True)
    own_rows = lax.dynamic_slice_in_dim(val_out_grad, first_row, quarter, 0)
    val_grad = (own_rows.astype(jnp.float32) + dx_rows).astype(jnp.bfloat16)
    attn_full, grad_full = (
        lax.all_gather(val_attn_inputs, "tok", axis=1, tiled=True),
        lax.all_gather(val_grad, "tok", axis=1, tiled=True),
    )
    total = pair_terms(
        train_inputs,
        train_grads,
        lax.all_gather(attn_full, "hid", axis=0, tiled=True),
        lax.all_gather(grad_full, "hid", axis=0, tiled=True),
    )
    influence = total / (train_inputs.shape[1] * math.sqrt(val_count))
    return (influence, val_grad)


def solution(mesh):
    placed = (
        P(None, "tok"),
        P(None, "tok"),
        P("tok", "hid"),
        P("tok", "hid"),
        P("hid", "tok"),
        P("hid", "tok"),
        P(("hid", "tok"), None),
        P(("hid", "tok"), None),
    )
    return jax.shard_map(
        local,
        mesh=mesh,
        in_specs=placed,
        out_specs=(P(("hid", "tok")), P("hid", "tok")),
        check_vma=False,
    )
```

profile of v0, /device:TPU:1, one launch (start us, length us, event | category | flops | bytes accessed | tf_op | source)
XLA Modules:
  0.0 1299.6 jit_solution(1939003087148605138)
XLA Ops:
  7.2 0.0 copy-start
  7.2 0.0 copy-start.3
  7.2 0.0 copy-start.1
  7.2 0.0 copy-start.4
  7.2 0.0 all-reduce.3.cloned.1.call-start
  7.3 1.8 fusion.13
  9.0 0.0 copy-done
  9.0 0.0 copy-done.3
  9.0 0.7 fusion.14
  9.7 0.0 copy-done.1
  9.7 0.0 copy-done.4
  9.7 0.7 fusion.15
  10.4 4.4 pad_maximum_fusion
  14.8 0.0 all-reduce.3.cloned.1.call-update
  14.8 0.0 all-gather.9.cloned.1.call-start
  14.8 0.6 copy-done.7
  15.4 0.6 dynamic-slice
  16.7 697.3 %all-reduce.3.cloned.1.call-done = f32[256,10752]{1,0:T(8,128)} async-done(((f32[256,10752]{1,0:T(8,128)}), f32[256,10752]{1,0:T(8,128)}) %all-reduce.3.cloned.1.call-update) | async-done | bytes 11010064
  713.9 1.1 fusion.11
  715.1 0.6 maximum_bitcast_fusion
  715.7 0.0 all-gather.9.cloned.1.call-update
  715.7 0.0 reduce-scatter.2.cloned.1.call-start
  715.8 0.1 copy.14
  715.9 0.0 copy-start.2
  715.9 162.7 %all-gather.9.cloned.1.call-done = bf16[64,4,7168]{2,1,0:T(4,128)(2,1)} async-done(((bf16[1,4,7168]{2,1,0:T(4,128)(2,1)}), bf16[64,4,7168]{2,1,0:T(4,128)(2,1)}) %all-gather.9.cloned.1.call-update) | async-done | bytes 3670032 | tf_op jit(solution)/shard_map/all_gather | solution.py:47
  878.6 6.7 reshape.5
  885.3 2.1 fusion
  887.4 0.0 copy-done.2
  887.4 2.8 fusion.6
  890.2 0.0 reduce-scatter.2.cloned.1.call-update
  890.2 0.0 all-gather.5.cloned.1.call-start
  890.3 155.9 %all_gather.15 = bf16[64,4096]{0,1:T(8,128)(2,1)S(1)} all-gather(bf16[64,64]{0,1:T(8,128)(2,1)S(1)} %copy.14), channel_id=1, replica_groups=mesh['hid'=4,'tok'=64] {'tok'}, dimensions={1}, use_global_device_ids=true | all-gather | bytes 532480 | tf_op jit(solution)/shard_map/all_gather | solution.py:55
  1046.2 1.1 copy.15
  1047.3 0.0 all-gather.5.cloned.1.call-update
  1047.3 0.0 all-gather.7.cloned.1.call-start
  1047.4 0.1 constant_dynamic-slice_fusion
  1047.5 0.1 copy.19
  1047.6 0.0 reduce-scatter.2.cloned.1.call-done
  1047.6 0.8 add_convert_fusion
  1048.4 0.1 copy.17
  1048.4 153.2 %all_gather.18 = bf16[64,4096]{0,1:T(8,128)(2,1)S(1)} all-gather(bf16[64,64]{0,1:T(8,128)(2,1)S(1)} %copy.17), channel_id=1, replica_groups=mesh['hid'=4,'tok'=64] {'tok'}, dimensions={1}, use_global_device_ids=true | all-gather | bytes 532480 | tf_op jit(solution)/shard_map/all_gather | solution.py:56
  1201.7 1.1 copy.18
  1202.8 0.0 all-gather.7.cloned.1.call-update
  1202.8 0.0 all-gather.5.cloned.1.call-done
  1202.9 5.0 fusion.12
  1207.9 79.7 %all-gather.7.cloned.1.call-done = bf16[256,4096]{1,0:T(8,128)(2,1)} async-done(((bf16[64,4096]{1,0:T(8,128)(2,1)}), bf16[256,4096]{1,0:T(8,128)(2,1)}) %all-gather.7.cloned.1.call-update) | async-done | bytes 2097168 | tf_op jit(solution)/shard_map/all_gather | solution.py:62
  1287.5 5.0 fusion.5
  1292.5 0.6 broadcast_multiply_fusion
  (5 shorter events, 0.0 us)
Async XLA Ops:
  7.2 1.9 copy-start
  7.2 1.8 copy-start.3
  7.2 2.5 copy-start.1
  7.2 2.5 copy-start.4
  7.2 706.7 %all-reduce.3.cloned.1.call-start = ((), (), s32[]{:S(2)}) async-start(), calls=%async_computation.5 | async-start | bytes 22020096
  14.8 0.7 copy-start.7
  14.8 701.0 %copy-start.6 = (bf16[64,64]{1,0:T(8,128)(2,1)S(1)}, bf16[64,64]{1,0:T(8,128)(2,1)}, u32[]{:S(2)}) copy-start(bf16[64,64]{1,0:T(8,128)(2,1)} %param.13) | copy-start | bytes 24580
  14.8 863.8 %all-gather.9.cloned.1.call-start = ((), (), s32[]{:S(2)}) async-start(), calls=%async_computation.4 | async-start | bytes 3727360 | tf_op jit(solution)/shard_map/all_gather | solution.py:47
  715.7 331.8 %reduce-scatter.2.cloned.1.call-start = ((), (), s32[]{:S(2)}) async-start(), calls=%async_computation.2 | async-start | bytes 163840 | tf_op jit(solution)/shard_map/reduce_scatter | solution.py:51
  715.9 171.5 %copy-start.2 = (bf16[64,3584]{1,0:T(8,128)(2,1)S(1)}, bf16[64,3584]{1,0:T(8,128)(2,1)}, u32[]{:S(2)}) copy-start(bf16[64,3584]{1,0:T(8,128)(2,1)} %param.10) | copy-start | bytes 1376260
  890.2 312.6 %all-gather.5.cloned.1.call-start = ((), (), s32[]{:S(2)}) async-start(), calls=%async_computation.1 | async-start | bytes 2621440 | tf_op jit(solution)/shard_map/all_gather | solution.py:61
  1047.3 240.2 %all-gather.7.cloned.1.call-start = ((), (), s32[]{:S(2)}) async-start(), calls=%async_computation.3 | async-start | bytes 2621440 | tf_op jit(solution)/shard_map/all_gather | solution.py:62
  1048.4 159.5 %copy-start.5 = (bf16[64,64]{1,0:T(8,128)(2,1)}, bf16[64,64]{1,0:T(8,128)(2,1)S(1)}, u32[]{:S(2)}) copy-start(bf16[64,64]{1,0:T(8,128)(2,1)S(1)} %add_convert_fusion) | copy-start | bytes 24580
Sparse Core Ops, SparseCore 0:
  14.9 698.9 all-reduce.2
  717.4 161.1 all-gather.8
  890.4 20.3 reduce-scatter.1
  1047.4 56.4 all-gather.4
  1203.0 84.5 all-gather.6
where the time goes:
time: 1300 us
  waiting for transfers between devices  940 us (72%)
  blocking collectives  309 us (24%)
  matrix products  17.9 us (1%)
  between operations  14.6 us (1%)
    unnamed x6, waiting for transfers between devices  697 us
    all_gather x1, waiting for transfers between devices, local(): piece = lax.all_gather(stacked, 'tok', axis=0, tiled=True)  163 us
    all_gather x1, blocking collectives, local(): lax.all_gather(val_attn_inputs, 'tok', axis=1, tiled=True)  156 us
    all_gather x1, blocking collectives, local(): lax.all_gather(val_grad, 'tok', axis=1, tiled=True)  153 us
    all_gather x1, waiting for transfers between devices, local(): lax.all_gather(grad_full, 'hid', axis=0, tiled=True)  79.7 us
  transfers between devices with their start and end apart: 5, of which 3 were waited for; matrix products, arithmetic and copies ran while one was open for 1% of the time, Pallas kernels for 0%

commit v1 on v0

--- a/solution.py
+++ b/solution.py
@@ -3,6 +3,13 @@
 import jax.numpy as jnp
 from jax import lax
 from jax.sharding import PartitionSpec as P
+
+
+def all_by_exchange(x, axis, dim):
+    size = lax.axis_size(axis)
+    shards = jnp.stack([x for _ in range(size)])
+    shards = lax.all_to_all(shards, axis, split_axis=0, concat_axis=0)
+    return jnp.concatenate(shards, axis=dim)
 
 
 def dot_rows(left, right):
@@ -52,7 +59,7 @@
     own_rows = lax.dynamic_slice_in_dim(val_out_grad, first_row, quarter, 0)
     val_grad = (own_rows.astype(jnp.float32) + dx_rows).astype(jnp.bfloat16)
     attn_full, grad_full = (
-        lax.all_gather(val_attn_inputs, "tok", axis=1, tiled=True),
+        all_by_exchange(val_attn_inputs, "tok", 1),
         lax.all_gather(val_grad, "tok", axis=1, tiled=True),
     )
     total = pair_terms(

time: 1300 us -> 1140 us (0.88)
  blocking collectives: 309 us -> 160 us
  waiting for transfers between devices: 940 us -> 915 us
    all_gather x1 -> x0, blocking collectives: 156 us -> none  [local(): lax.all_gather(val_attn_inputs, 'tok', axis=1, tiled=True)]
    all_gather x1, waiting for transfers between devices: 79.7 us -> 46.1 us  [local(): lax.all_gather(grad_full, 'hid', axis=0, tiled=True)]
    reduce_scatter x1, waiting for transfers between devices: 0.02 us -> 17.3 us  [local(): dx_rows = lax.psum_scatter(dx_part, 'hid', scatter_dimension=0, tiled=True)]
  transfers between devices with their start and end apart: 5 -> 6, of which waited for: 3 -> 4; matrix products, arithmetic and copies ran while one was open for 1% -> 2% of each run, Pallas kernels for 0% -> 0%
where the time goes in v1:
time: 1140 us
  waiting for transfers between devices  915 us (80%)
  blocking collectives  160 us (14%)
  matrix products  17.9 us (2%)
  between operations  14.6 us (1%)
  local copies, waits for them, and re-layouts  14.1 us (1%)
    unnamed x6, waiting for transfers between devices  697 us
    all_gather x1, blocking collectives, local(): lax.all_gather(val_grad, 'tok', axis=1, tiled=True)  160 us
    all_gather x1, waiting for transfers between devices, local(): piece = lax.all_gather(stacked, 'tok', axis=0, tiled=True)  155 us
    all_gather x1, waiting for transfers between devices, local(): lax.all_gather(grad_full, 'hid', axis=0, tiled=True)  46.1 us
  transfers between devices with their start and end apart: 6, of which 4 were waited for; matrix products, arithmetic and copies ran while one was open for 2% of the time, Pallas kernels for 0%

profile of v1, /device:TPU:1, one launch (start us, length us, event | category | flops | bytes accessed | tf_op | source)
XLA Modules:
  0.0 1137.2 jit_solution(18255794344701324148)
XLA Ops:
  7.2 0.0 copy-start
  7.2 0.0 copy-start.3
  7.2 0.0 copy-start.1
  7.2 0.0 copy-start.4
  7.2 0.0 all-reduce.3.cloned.1.call-start
  7.3 1.8 fusion.13
  9.0 0.0 copy-done
  9.0 0.7 fusion.14
  9.7 0.7 fusion.15
  10.4 4.4 pad_maximum_fusion
  14.8 0.0 all-reduce.3.cloned.1.call-update
  14.8 0.0 all-gather.9.cloned.1.call-start
  14.8 0.6 copy-done.7
  15.4 0.6 dynamic-slice
  16.7 697.3 %all-reduce.3.cloned.1.call-done = f32[256,10752]{1,0:T(8,128)} async-done(((f32[256,10752]{1,0:T(8,128)}), f32[256,10752]{1,0:T(8,128)}) %all-reduce.3.cloned.1.call-update) | async-done | bytes 11010064
  713.9 1.1 fusion.11
  715.1 0.6 maximum_bitcast_fusion
  715.7 0.0 all-gather.9.cloned.1.call-update
  715.7 0.2 stack.2
  716.0 1.5 reshape.17
  717.5 7.7 all-to-all-start
  725.3 0.0 copy-start.2
  725.3 0.0 reduce-scatter.2.cloned.1.call-start
  725.4 154.7 %all-gather.9.cloned.1.call-done = bf16[64,4,7168]{2,1,0:T(4,128)(2,1)} async-done(((bf16[1,4,7168]{2,1,0:T(4,128)(2,1)}), bf16[64,4,7168]{2,1,0:T(4,128)(2,1)}) %all-gather.9.cloned.1.call-update) | async-done | bytes 3670032 | tf_op jit(solution)/shard_map/all_gather | solution.py:54
  880.0 6.7 reshape.15
  886.7 2.1 fusion
  888.9 2.8 fusion.6
  891.6 0.0 reduce-scatter.2.cloned.1.call-update
  891.7 0.0 all-gather.5.cloned.1.call-start
  891.7 0.0 all-to-all-done
  891.7 0.7 reshape.18
  892.4 0.7 copy.15
  893.1 1.6 reshape.13
  894.7 0.0 all-gather.5.cloned.1.call-update
  894.7 0.0 all-gather.7.cloned.1.call-start
  894.8 0.1 constant_dynamic-slice_fusion
  894.9 0.1 copy.19
  895.0 17.3 %reduce-scatter.2.cloned.1.call-done = f32[64,64]{1,0:T(8,128)} async-done(((f32[256,64]{1,0:T(8,128)}), f32[64,64]{1,0:T(8,128)}) %reduce-scatter.2.cloned.1.call-update) | async-done | bytes 16400 | tf_op jit(solution)/shard_map/reduce_scatter | solution.py:58
  912.2 0.8 add_convert_fusion
  913.0 0.1 copy.17
  913.1 159.8 %all_gather.14 = bf16[64,4096]{0,1:T(8,128)(2,1)S(1)} all-gather(bf16[64,64]{0,1:T(8,128)(2,1)S(1)} %copy.17), channel_id=1, replica_groups=mesh['hid'=4,'tok'=64] {'tok'}, dimensions={1}, use_global_device_ids=true | all-gather | bytes 532480 | tf_op jit(solution)/shard_map/all_gather | solution.py:63
  1072.9 1.1 copy.18
  1074.0 0.0 all-gather.7.cloned.1.call-update
  1074.1 0.0 all-gather.5.cloned.1.call-done
  1074.1 5.0 fusion.12
  1079.1 46.1 %all-gather.7.cloned.1.call-done = bf16[256,4096]{1,0:T(8,128)(2,1)} async-done(((bf16[64,4096]{1,0:T(8,128)(2,1)}), bf16[256,4096]{1,0:T(8,128)(2,1)}) %all-gather.7.cloned.1.call-update) | async-done | bytes 2097168 | tf_op jit(solution)/shard_map/all_gather | solution.py:69
  1125.1 5.0 fusion.5
  1130.1 0.6 broadcast_multiply_fusion
  (9 shorter events, 0.0 us)
Async XLA Ops:
  7.2 1.9 copy-start
  7.2 1.8 copy-start.3
  7.2 2.5 copy-start.1
  7.2 2.5 copy-start.4
  7.2 706.7 %all-reduce.3.cloned.1.call-start = ((), (), s32[]{:S(2)}) async-start(), calls=%async_computation.6 | async-start | bytes 22020096
  14.7 0.7 copy-start.7
  14.8 701.0 %copy-start.6 = (bf16[64,64]{1,0:T(8,128)(2,1)S(1)}, bf16[64,64]{1,0:T(8,128)(2,1)}, u32[]{:S(2)}) copy-start(bf16[64,64]{1,0:T(8,128)(2,1)} %param.13) | copy-start | bytes 24580
  14.8 865.2 %all-gather.9.cloned.1.call-start = ((), (), s32[]{:S(2)}) async-start(), calls=%async_computation.5 | async-start | bytes 3727360 | tf_op jit(solution)/shard_map/all_gather | solution.py:54
  717.5 174.2 %all-to-all-start = ((bf16[64,2,2048]{2,1,0:T(2,128)(2,1)}), bf16[64,2,2048]{2,1,0:T(2,128)(2,1)S(1)}, u32[]{:S(2)}, u32[]{:S(2)}) async-start(bf16[64,2,2048]{2,1,0:T(2,128)(2,1)} %reshape.17), calls=%async_computation | async-start | bytes 1048576 | tf_op jit(solution)/shard_map/all_to_all | solution.py:11
  725.3 163.6 %copy-start.2 = (bf16[64,3584]{1,0:T(8,128)(2,1)S(1)}, bf16[64,3584]{1,0:T(8,128)(2,1)}, u32[]{:S(2)}) copy-start(bf16[64,3584]{1,0:T(8,128)(2,1)} %param.10) | copy-start | bytes 1376260
  725.3 186.9 %reduce-scatter.2.cloned.1.call-start = ((), (), s32[]{:S(2)}) async-start(), calls=%async_computation.3 | async-start | bytes 163840 | tf_op jit(solution)/shard_map/reduce_scatter | solution.py:58
  891.7 182.4 %all-gather.5.cloned.1.call-start = ((), (), s32[]{:S(2)}) async-start(), calls=%async_computation.2 | async-start | bytes 2621440 | tf_op jit(solution)/shard_map/all_gather | solution.py:68
  894.7 230.4 %all-gather.7.cloned.1.call-start = ((), (), s32[]{:S(2)}) async-start(), calls=%async_computation.4 | async-start | bytes 2621440 | tf_op jit(solution)/shard_map/all_gather | solution.py:69
  913.0 166.1 %copy-start.5 = (bf16[64,64]{1,0:T(8,128)(2,1)}, bf16[64,64]{1,0:T(8,128)(2,1)S(1)}, u32[]{:S(2)}) copy-start(bf16[64,64]{1,0:T(8,128)(2,1)S(1)} %add_convert_fusion) | copy-start | bytes 24580
Sparse Core Ops, SparseCore 0:
  14.9 698.9 all-reduce.2
  717.4 162.5 all-gather.8
  891.8 20.3 reduce-scatter.1
  913.9 32.7 all-gather.4
  1074.2 50.9 all-gather.6
